TPU v7x, 512 devices: a whole 4x8x8 slice. The times are simulated.
512 devices in a mesh: row: 16 (over z, y_lo), col: 4 (over x), seq: 8 (over y_hi, core).
Axes of the slice: x: 4, y: 8 (y_hi: 4, y_lo: 2; y = y_hi * 2 + y_lo), z: 8, core: 2. Of those that a mesh axis runs over, the one named last changes fastest.
Arguments:
- pair: bfloat16 [1024, 1024, 128], P(('row', 'seq'), 'col'), may hold values from -6 to 6
- alignment: bfloat16 [128, 1024, 256], P(('row', 'seq'), 'col'), may hold values from -6 to 6
- opm_left: bfloat16 [256, 32], replicated, may hold values from -0.375 to 0.375
- opm_right: bfloat16 [256, 32], replicated, may hold values from -0.375 to 0.375
- opm_out: bfloat16 [1024, 128], replicated, may hold values from -2 to 2
- tri_left: bfloat16 [128, 128], replicated, may hold values from -0.5 to 0.5
- tri_left_gate: bfloat16 [128, 128], replicated, may hold values from -0.5 to 0.5
- tri_right: bfloat16 [128, 128], replicated, may hold values from -0.5 to 0.5
- tri_right_gate: bfloat16 [128, 128], replicated, may hold values from -0.5 to 0.5
- tri_gate: bfloat16 [128, 128], replicated, may hold values from -0.5 to 0.5
- tri_out: bfloat16 [128, 128], replicated, may hold values from -0.5 to 0.5
Outputs:
- pair_out: bfloat16 [1024, 1024, 128], P(('row', 'seq'), 'col')
All inputs are finite; a program needn't handle non-finite values.
Results may differ from a plain program's by a relative error of at most 0.0075.
Values may be sent and summed in bfloat16 or wider, within the bound.
A program may use at most 64 MiB of HBM per device.

v0:
```python
import jax
import jax.numpy as jnp
from jax import lax
from jax.sharding import PartitionSpec as P

EPS = 1e-05


def spread_2(shard, axis, root):
    mine = lax.axis_index(axis) == root
    return lax.psum(jnp.where(mine, shard, jnp.zeros_like(shard)), axis)


def layer_norm(values, axis):
    values = values.astype(jnp.float32)
    center = values - jnp.mean(values, axis=axis, keepdims=True)
    spread = jnp.mean(center * center, axis=axis, keepdims=True)
    return center * lax.rsqrt(spread + EPS)


def contract(local_rows, piece):
    return jnp.einsum("cik,cjk->cij", local_rows, piece, preferred_element_type=jnp.float32)


def on_device(
    pair,
    alignment,
    opm_left,
    opm_right,
    opm_out,
    tri_left,
    tri_left_gate,
    tri_right,
    tri_right_gate,
    tri_gate,
    tri_out,
):
    rows_here, cols_here, pair_width = pair.shape
    seq_here = alignment.shape[0]
    model_width = alignment.shape[2]
    factor_width = opm_left.shape[1]
    hidden = tri_left.shape[1]
    n_row = lax.axis_size("row")
    n_col = lax.axis_size("col")
    n_seq = lax.axis_size("seq")
    seq_normed = (
        layer_norm(alignment, 2).astype(jnp.bfloat16).reshape(seq_here * cols_here, model_width)
    )
    left_proj = (
        jnp.dot(seq_normed, opm_left, preferred_element_type=jnp.float32)
        .astype(jnp.bfloat16)
        .reshape(seq_here, cols_here * factor_width)
    )
    right_proj = (
        jnp.dot(seq_normed, opm_right, preferred_element_type=jnp.float32)
        .astype(jnp.bfloat16)
        .reshape(seq_here, cols_here * factor_width)
    )
    per_col = n_row // n_col
    index_row = lax.axis_index("row")
    root_col = index_row // per_col
    left_all, right_all = (
        lax.all_gather(left_proj, ("row", "seq"), axis=0, tiled=True),
        lax.all_gather(right_proj, ("row", "seq"), axis=0, tiled=True),
    )
    index_seq = lax.axis_index("seq")
    offset = (index_row % per_col * n_seq + index_seq) * (rows_here * factor_width)
    row_slice = lax.dynamic_slice_in_dim(left_all, offset, rows_here * factor_width, 1)
    seqs_all = right_all.shape[0]
    row_factors = spread_2(row_slice, "col", root_col)
    right_wide = right_all.reshape(seqs_all, cols_here, factor_width)
    row_stack = jnp.swapaxes(row_factors.reshape(seqs_all, rows_here, factor_width), 0, 1)

    def outer_row(packed):
        row_vals, pair_row = packed
        outer_sum = jnp.einsum(
            "np,njq->jpq", row_vals, right_wide, preferred_element_type=jnp.float32
        )
        mean_outer = (
            (outer_sum * (1.0 / seqs_all))
            .astype(jnp.bfloat16)
            .reshape(cols_here, factor_width * factor_width)
        )
        return (
            pair_row.astype(jnp.float32)
            + jnp.dot(mean_outer, opm_out, preferred_element_type=jnp.float32)
        ).astype(jnp.bfloat16)

    pair_mid = lax.map(outer_row, (row_stack, pair))
    normed_pair = layer_norm(pair_mid, 2).astype(jnp.bfloat16)
    flat_pair = normed_pair.reshape(rows_here * cols_here, pair_width)

    def project(weight):
        return lax.dot_general(
            weight, flat_pair, (((0,), (1,)), ((), ())), preferred_element_type=jnp.float32
        )

    def gated(weight_gate, weight_value):
        gate_part = jax.nn.sigmoid(project(weight_gate))
        return (
            (gate_part * project(weight_value))
            .astype(jnp.bfloat16)
            .reshape(hidden, rows_here, cols_here)
        )

    left_first = gated(tri_left_gate, tri_left)
    right_first = gated(tri_right_gate, tri_right)
    left_local, right_local = (
        lax.all_to_all(
            lax.all_to_all(left_first, "col", split_axis=0, concat_axis=2, tiled=True),
            "seq",
            split_axis=0,
            concat_axis=1,
            tiled=True,
        ),
        lax.all_to_all(
            lax.all_to_all(right_first, "col", split_axis=0, concat_axis=2, tiled=True),
            "seq",
            split_axis=0,
            concat_axis=1,
            tiled=True,
        ),
    )
    product = contract(left_local, lax.all_gather(right_local, "row", axis=1, tiled=True))
    product = product.astype(jnp.bfloat16)
    returned = lax.all_to_all(
        lax.all_to_all(product, "col", split_axis=2, concat_axis=0, tiled=True),
        "seq",
        split_axis=1,
        concat_axis=0,
        tiled=True,
    )
    per_group = hidden // (n_col * n_seq)
    weights_order = (
        tri_out.reshape(n_col, n_seq, per_group, pair_width)
        .transpose(1, 0, 2, 3)
        .reshape(hidden, pair_width)
    )
    normed_product = layer_norm(returned, 0).astype(jnp.bfloat16)
    update = jnp.einsum(
        "cij,cd->ijd", normed_product, weights_order, preferred_element_type=jnp.float32
    )
    gate_part = jax.nn.sigmoid(
        jnp.dot(flat_pair, tri_gate, preferred_element_type=jnp.float32)
    ).reshape(rows_here, cols_here, pair_width)
    return (pair_mid.astype(jnp.float32) + gate_part * update).astype(jnp.bfloat16)


def solution(mesh):
    return jax.shard_map(
        on_device,
        mesh=mesh,
        in_specs=(
            P(("row", "seq"), "col", None),
            P(("row", "seq"), "col", None),
            P(),
            P(),
            P(),
            P(),
            P(),
            P(),
            P(),
            P(),
            P(),
        ),
        out_specs=P(("row", "seq"), "col", None),
        check_vma=False,
    )
```

profile of v0, /device:TPU:8, one launch (start us, length us, event | category | flops | bytes accessed | tf_op | source)
XLA Modules:
  0.0 817.1 jit_solution(16406924209503788000)
XLA Ops:
  8.7 1.2 convolution_convert_fusion.2
  10.8 1.2 convolution_convert_fusion.1
  12.9 222.3 %all-gather.8.cloned.1.call-done = bf16[128,1,8192]{2,1,0:T(2,128)(2,1)} async-done(((bf16[1,1,8192]{2,1,0:T(2,128)(2,1)}), bf16[128,1,8192]{2,1,0:T(2,128)(2,1)}) %all-gather.8.cloned.1.call-update) | async-done | bytes 2097168 | tf_op jit(solution)/shard_map/all_gather | solution.py:63
  237.1 218.4 %all-gather.10.cloned.1.call-done = bf16[128,1,8192]{2,1,0:T(2,128)(2,1)} async-done(((bf16[1,1,8192]{2,1,0:T(2,128)(2,1)}), bf16[128,1,8192]{2,1,0:T(2,128)(2,1)}) %all-gather.10.cloned.1.call-update) | async-done | bytes 2097168 | tf_op jit(solution)/shard_map/all_gather | solution.py:64
  455.5 9.1 %copy.67 = bf16[128,1,8192]{0,2,1:T(8,128)(2,1)} copy(bf16[128,1,8192]{2,1,0:T(2,128)(2,1)} %all-gather.10.cloned.1.call-done) | data formatting | bytes 4194304 | tf_op jit(solution)/shard_map/all_gather | solution.py:64
  464.7 3.0 copy.68
  467.7 40.3 %all-reduce.2.cloned.1.call-done = bf16[8,128,32]{1,2,0:T(8,128)(2,1)} async-done(((bf16[8,128,32]{1,2,0:T(8,128)(2,1)}), bf16[8,128,32]{1,2,0:T(8,128)(2,1)}) %all-reduce.2.cloned.1.call-update) | async-done | bytes 65552 | tf_op jit(solution)/shard_map/psum | solution.py:11
  508.0 21.1 %while.10 = (s32[]{:T(128)}, bf16[8,256,128]{2,1,0:T(8,128)(2,1)S(1)}, bf16[8,256,128]{2,1,0:T(8,128)(2,1)}, bf16[8,128,32]{1,2,0:T(8,128)(2,1)}, bf16[128,256,3...) while((s32[]{:T(128)}, bf16[8,256,128]{2,1,0:T(8,128)(2,1)S(1)}, ...), condition=%wide.region_4.5_spmd, body=%wide.region_3.4_spmd.sunk | while | flops 134840320 | bytes 4596305 | solution.py:89
  509.4 1.2 fusion.68
  510.7 1.1 fusion.67
  512.1 1.2 fusion.68
  513.3 1.1 fusion.67
  514.7 1.2 fusion.68
  516.0 1.1 fusion.67
  517.4 1.2 fusion.68
  518.6 1.1 fusion.67
  520.0 1.2 fusion.68
  521.2 1.1 fusion.67
  522.7 1.2 fusion.68
  523.9 1.1 fusion.67
  525.3 1.2 fusion.68
  528.0 1.2 fusion.68
  531.8 11.3 %all_to_all.99 = bf16[128,8,256]{2,1,0:T(8,128)(2,1)S(1)} all-to-all(bf16[128,8,256]{2,1,0:T(8,128)(2,1)S(1)} %copy.72), channel_id=1, replica_groups=mesh['row'=16,'col'=4,'seq'=8] {'col'}, dimensions={0} | all-to-all | bytes 1048576 | tf_op jit(solution)/shard_map/all_to_all | solution.py:117
  543.2 24.0 %all_to_all.100 = bf16[32,8,1024]{2,1,0:T(8,128)(2,1)S(1)} all-to-all(bf16[32,8,1024]{2,1,0:T(8,128)(2,1)S(1)} %bitcast.131), channel_id=1, replica_groups=mesh['row'=16,'col'=4,'seq'=8] {'seq'}, dimensions={0} | all-to-all | bytes 1048576 | tf_op jit(solution)/shard_map/all_to_all | solution.py:116
  569.1 10.5 %all_to_all.101 = bf16[128,8,256]{2,1,0:T(8,128)(2,1)S(1)} all-to-all(bf16[128,8,256]{2,1,0:T(8,128)(2,1)S(1)} %copy.69), channel_id=1, replica_groups=mesh['row'=16,'col'=4,'seq'=8] {'col'}, dimensions={0} | all-to-all | bytes 1048576 | tf_op jit(solution)/shard_map/all_to_all | solution.py:110
  579.7 26.7 %all_to_all.102 = bf16[32,8,1024]{2,1,0:T(8,128)(2,1)S(1)} all-to-all(bf16[32,8,1024]{2,1,0:T(8,128)(2,1)S(1)} %bitcast.134), channel_id=1, replica_groups=mesh['row'=16,'col'=4,'seq'=8] {'seq'}, dimensions={0} | all-to-all | bytes 1048576 | tf_op jit(solution)/shard_map/all_to_all | solution.py:109
  606.4 153.9 %all-gather.6.cloned.1.call-done = bf16[4,1024,1024]{2,1,0:T(8,128)(2,1)} async-done(((bf16[4,64,1024]{2,1,0:T(8,128)(2,1)}), bf16[4,1024,1024]{2,1,0:T(8,128)(2,1)}) %all-gather.6.cloned.1.call-update) | async-done | bytes 8388624 | tf_op jit(solution)/shard_map/all_gather | solution.py:124
  760.3 6.0 convolution_convert_fusion
  767.9 13.4 %all_to_all.103 = bf16[4,2,32768]{2,1,0:T(2,128)(2,1)S(1)} all-to-all(bf16[4,2,32768]{2,1,0:T(2,128)(2,1)S(1)} %reshape.114), channel_id=1, replica_groups=mesh['row'=16,'col'=4,'seq'=8] {'col'}, dimensions={0} | all-to-all | bytes 1048576 | tf_op jit(solution)/shard_map/all_to_all | solution.py:127
  783.6 6.7 all-to-all-start.5
  790.8 17.9 %all-to-all-done.5 = bf16[16,64,256]{2,0,1:T(8,128)(2,1)S(1)} async-done(((bf16[16,64,256]{2,0,1:T(8,128)(2,1)}), bf16[16,64,256]{2,0,1:T(8,128)(2,1)S(1)}, u32[]{:S(2)}, u32[]{:S(2)}) %all-to-all-start.5) | async-done | bytes 524320 | tf_op jit(solution)/shard_map/all_to_all | solution.py:126
  809.4 1.1 fusion.19
  (71 shorter events, 20.1 us)
Async XLA Ops:
  6.5 524.1 %copy-start = (bf16[128,128]{1,0:T(8,128)(2,1)S(1)}, bf16[128,128]{1,0:T(8,128)(2,1)}, u32[]{:S(2)}) copy-start(bf16[128,128]{1,0:T(8,128)(2,1)} %param.21) | copy-start | bytes 98308
  6.5 228.7 %all-gather.8.cloned.1.call-start = ((), (), s32[]{:S(2)}) async-start(), calls=%async_computation.8 | async-start | bytes 4227072 | tf_op jit(solution)/shard_map/all_gather | solution.py:63
  10.7 444.8 %all-gather.10.cloned.1.call-start = ((), (), s32[]{:S(2)}) async-start(), calls=%async_computation.9 | async-start | bytes 4227072 | tf_op jit(solution)/shard_map/all_gather | solution.py:64
  12.8 495.2 %all-reduce.2.cloned.1.call-start = ((), (), s32[]{:S(2)}) async-start(), calls=%async_computation.6 | async-start | bytes 131072 | tf_op jit(solution)/shard_map/psum | solution.py:11
  237.1 523.2 %all-gather.6.cloned.1.call-start = ((), (), s32[]{:S(2)}) async-start(), calls=%async_computation.7 | async-start | bytes 8912896 | tf_op jit(solution)/shard_map/all_gather | solution.py:124
  237.1 270.9 %copy-start.1 = (bf16[1024,128]{1,0:T(8,128)(2,1)S(1)}, bf16[1024,128]{1,0:T(8,128)(2,1)}, u32[]{:S(2)}) copy-start(bf16[1024,128]{1,0:T(8,128)(2,1)} %param.17) | copy-start | bytes 786436
  529.2 1.9 copy-start.2
  531.1 36.9 %copy-start.5 = (bf16[128,128]{1,0:T(8,128)(2,1)S(1)}, bf16[128,128]{1,0:T(8,128)(2,1)}, u32[]{:S(2)}) copy-start(bf16[128,128]{1,0:T(8,128)(2,1)} %param.19) | copy-start | bytes 98308
  543.1 25.3 %copy-start.3 = (bf16[128,128]{1,0:T(8,128)(2,1)S(1)}, bf16[128,128]{1,0:T(8,128)(2,1)}, u32[]{:S(2)}) copy-start(bf16[128,128]{1,0:T(8,128)(2,1)} %param.18) | copy-start | bytes 98308
  767.0 23.3 %copy-start.4 = (bf16[128,128]{1,0:T(8,128)(2,1)S(1)}, bf16[128,128]{1,0:T(8,128)(2,1)}, u32[]{:S(2)}) copy-start(bf16[128,128]{1,0:T(8,128)(2,1)} %param.23) | copy-start | bytes 98308
  767.0 23.4 %copy-start.6 = (bf16[128,128]{1,0:T(8,128)(2,1)S(1)}, bf16[128,128]{1,0:T(8,128)(2,1)}, u32[]{:S(2)}) copy-start(bf16[128,128]{1,0:T(8,128)(2,1)} %param.22) | copy-start | bytes 98308
  783.6 25.1 %all-to-all-start.5 = ((bf16[16,64,256]{2,0,1:T(8,128)(2,1)}), bf16[16,64,256]{2,0,1:T(8,128)(2,1)S(1)}, u32[]{:S(2)}, u32[]{:S(2)}) async-start(bf16[16,64,256]{2,0,1:T(8,128)(2,1)} %copy.78), calls=%async_computation.5 | async-start | bytes 1048576 | tf_op jit(solution)/shard_map/all_to_all | solution.py:126
Sparse Core Ops, SparseCore 0:
  10.8 224.3 all-gather.7
  237.4 218.1 all-gather.9
  457.9 50.1 all-reduce.1
  568.1 192.1 all-gather.5
where the time goes:
time: 819 us; the launch traced here: 817 us
  waiting for transfers between devices  653 us (80%)
  blocking collectives  85.8 us (10%)
  matrix products  29.9 us (4%)
  local copies, waits for them, and re-layouts  23.1 us (3%)
  between operations  13.5 us (2%)
    all_gather x1, waiting for transfers between devices, on_device(): lax.all_gather(left_proj, ('row', 'seq'), axis=0, tiled=True)  222 us
    all_gather x1, waiting for transfers between devices, on_device(): lax.all_gather(right_proj, ('row', 'seq'), axis=0, tiled=True)  218 us
    all_gather x1, waiting for transfers between devices, on_device(): lax.all_gather(right_local, 'row', axis=1, tiled=True)  154 us
    psum x1, waiting for transfers between devices, spread_2(): return lax.psum(jnp.where(mine, shard, jnp.zeros_like(shard)), axis)  40.3 us
    all_to_all x1, blocking collectives, on_device(): lax.all_to_all(lax.all_to_all(left_first, 'col', split_axis=0, concat_axi...  26.7 us
    all_to_all x1, blocking collectives, on_device(): lax.all_to_all(lax.all_to_all(right_first, 'col', split_axis=0, concat_ax...  24 us
    all_to_all x1, waiting for transfers between devices, on_device(): lax.all_to_all(lax.all_to_all(product, 'col', split_axis=2, concat_axis=0...  17.9 us
  transfers between devices with their start and end apart: 5, of which 5 were waited for; matrix products, arithmetic and copies ran while one was open for 2% of the time, Pallas kernels for 0%

commit v1 on v0

--- a/solution.py
+++ b/solution.py
@@ -60,7 +60,12 @@
     index_row = lax.axis_index("row")
     root_col = index_row // per_col
     left_all, right_all = (
-        lax.all_gather(left_proj, ("row", "seq"), axis=0, tiled=True),
+        jnp.concatenate(
+            lax.all_to_all(
+                jnp.stack([left_proj] * lax.axis_size(("row", "seq"))), ("row", "seq"), 0, 0
+            ),
+            axis=0,
+        ),
         lax.all_gather(right_proj, ("row", "seq"), axis=0, tiled=True),
     )
     index_seq = lax.axis_index("seq")

time: 819 us -> 616 us (0.75)
  waiting for transfers between devices: 653 us -> 400 us
  starting transfers between devices: 6.87 us -> 24.2 us
  local copies, waits for them, and re-layouts: 23.1 us -> 38.7 us
  other arithmetic: 4.87 us -> 18.1 us
    all_gather x1 -> x0, waiting for transfers between devices: 222 us -> none  [on_device(): lax.all_gather(left_proj, ('row', 'seq'), axis=0, tiled=True)]
    all_to_all x0 -> x1, waiting for transfers between devices: none -> 51.6 us  [on_device(): lax.all_to_all(jnp.stack([left_proj] * lax.axis_size(('row', 'seq'))), ('...]
    all_gather x1, waiting for transfers between devices: 218 us -> 178 us  [on_device(): lax.all_gather(right_proj, ('row', 'seq'), axis=0, tiled=True)]
    psum x1, waiting for transfers between devices: 40.3 us -> 0.03 us  [spread_2(): return lax.psum(jnp.where(mine, shard, jnp.zeros_like(shard)), axis)]
    all_to_all x0 -> x1, starting transfers between devices: none -> 17.4 us  [on_device(): lax.all_to_all(jnp.stack([left_proj] * lax.axis_size(('row', 'seq'))), ('...]
    another operation x0 -> x1, other arithmetic: none -> 13.2 us  [on_device(): jnp.stack([left_proj] * lax.axis_size(('row', 'seq')))]
    unnamed x19 -> x24, local copies, waits for them, and re-layouts: 3.2 us -> 12 us
  transfers between devices with their start and end apart: 5 -> 5, of which waited for: 5 -> 4; matrix products, arithmetic and copies ran while one was open for 2% -> 4% of each run, Pallas kernels for 0% -> 0%
where the time goes in v1:
time: 616 us; the launch traced here: 614 us
  waiting for transfers between devices  400 us (65%)
  blocking collectives  85.9 us (14%)
  local copies, waits for them, and re-layouts  38.7 us (6%)
  matrix products  31.2 us (5%)
  starting transfers between devices  24.2 us (4%)
  other arithmetic  18.1 us (3%)
  between operations  15.2 us (2%)
    all_gather x1, waiting for transfers between devices, on_device(): lax.all_gather(right_proj, ('row', 'seq'), axis=0, tiled=True)  178 us
    all_gather x1, waiting for transfers between devices, on_device(): lax.all_gather(right_local, 'row', axis=1, tiled=True)  154 us
    all_to_all x1, waiting for transfers between devices, on_device(): lax.all_to_all(jnp.stack([left_proj] * lax.axis_size(('row', 'seq'))), ('...  51.6 us
    all_to_all x1, blocking collectives, on_device(): lax.all_to_all(lax.all_to_all(left_first, 'col', split_axis=0, concat_axi...  25.9 us
    all_to_all x1, blocking collectives, on_device(): lax.all_to_all(lax.all_to_all(right_first, 'col', split_axis=0, concat_ax...  21.5 us
    all_to_all x1, starting transfers between devices, on_device(): lax.all_to_all(jnp.stack([left_proj] * lax.axis_size(('row', 'seq'))), ('...  17.4 us
    all_to_all x1, waiting for transfers between devices, on_device(): lax.all_to_all(lax.all_to_all(product, 'col', split_axis=2, concat_axis=0...  16.9 us
    all_to_all x1, blocking collectives, on_device(): lax.all_to_all(right_first, 'col', split_axis=0, concat_axis=2, tiled=True)  13.4 us
  transfers between devices with their start and end apart: 5, of which 4 were waited for; matrix products, arithmetic and copies ran while one was open for 4% of the time, Pallas kernels for 0%

profile of v1, /device:TPU:8, one launch (start us, length us, event | category | flops | bytes accessed | tf_op | source)
XLA Modules:
  0.0 613.9 jit_solution(3190073703241617097)
XLA Ops:
  9.5 1.2 convolution_convert_fusion.2
  10.9 6.1 stack.3
  17.5 13.2 %reduce.4 = bf16[128,8192]{1,0:T(8,128)(2,1)S(1)} reduce(bf16[128,1,8192]{2,1,0:T(2,128)(2,1)} %stack.3, bf16[]{:T(256)} %broadcast.99), dimensions={1}, to_apply=%stack.3.reduce_sub_computation | reduce | bytes 4194306 | tf_op jit(solution)/shard_map/stack | solution.py:65
  30.8 2.8 reshape.112
  33.6 17.4 %all-to-all-start = ((bf16[128,2,4096]{2,1,0:T(2,128)(2,1)}), bf16[128,2,4096]{2,1,0:T(2,128)(2,1)S(1)}, u32[]{:S(2)}, u32[]{:S(2)}) async-start(bf16[128,2,4096]{2,1,0:T(2,128)(2,1)} %reshape.112), calls=%async_computation | async-start | bytes 4194304 | tf_op jit(solution)/shard_map/all_to_all | solution.py:64
  52.2 51.6 %all-to-all-done = bf16[128,2,4096]{2,1,0:T(2,128)(2,1)S(1)} async-done(((bf16[128,2,4096]{2,1,0:T(2,128)(2,1)}), bf16[128,2,4096]{2,1,0:T(2,128)(2,1)S(1)}, u32[]{:S(2)}, u32[]{:S(2)}) %all-to-all-start) | async-done | bytes 2097184 | tf_op jit(solution)/shard_map/all_to_all | solution.py:64
  103.8 6.8 %reshape.113 = bf16[128,1,8192]{2,1,0:T(2,128)(2,1)} reshape(bf16[128,2,4096]{2,1,0:T(2,128)(2,1)S(1)} %all-to-all-done) | data formatting | bytes 4194304
  112.5 178.0 %all-gather.6.cloned.1.call-done = bf16[128,1,8192]{2,1,0:T(2,128)(2,1)} async-done(((bf16[1,1,8192]{2,1,0:T(2,128)(2,1)}), bf16[128,1,8192]{2,1,0:T(2,128)(2,1)}) %all-gather.6.cloned.1.call-update) | async-done | bytes 2097168 | tf_op jit(solution)/shard_map/all_gather | solution.py:69
  290.5 9.1 %copy.50 = bf16[128,1,8192]{0,2,1:T(8,128)(2,1)} copy(bf16[128,1,8192]{2,1,0:T(2,128)(2,1)} %all-gather.6.cloned.1.call-done) | data formatting | bytes 4194304 | tf_op jit(solution)/shard_map/all_gather | solution.py:69
  299.6 3.0 copy.51
  302.7 21.2 %while.10 = (s32[]{:T(128)}, bf16[8,256,128]{2,1,0:T(8,128)(2,1)S(1)}, bf16[8,256,128]{2,1,0:T(8,128)(2,1)}, bf16[8,128,32]{1,2,0:T(8,128)(2,1)}, bf16[128,256,3...) while((s32[]{:T(128)}, bf16[8,256,128]{2,1,0:T(8,128)(2,1)S(1)}, ...), condition=%wide.region_4.5_spmd, body=%wide.region_3.4_spmd.sunk | while | flops 134840320 | bytes 4596305 | solution.py:94
  302.7 1.1 fusion.67
  304.1 1.2 fusion.68
  305.3 1.1 fusion.67
  306.7 1.2 fusion.68
  309.4 1.2 fusion.68
  312.0 1.2 fusion.68
  314.7 1.2 fusion.68
  317.3 1.2 fusion.68
  320.0 1.2 fusion.68
  322.6 1.2 fusion.68
  326.5 13.4 %all_to_all.104 = bf16[128,8,256]{2,1,0:T(8,128)(2,1)S(1)} all-to-all(bf16[128,8,256]{2,1,0:T(8,128)(2,1)S(1)} %copy.55), channel_id=1, replica_groups=mesh['row'=16,'col'=4,'seq'=8] {'col'}, dimensions={0} | all-to-all | bytes 1048576 | tf_op jit(solution)/shard_map/all_to_all | solution.py:122
  340.0 21.5 %all_to_all.105 = bf16[32,8,1024]{2,1,0:T(8,128)(2,1)S(1)} all-to-all(bf16[32,8,1024]{2,1,0:T(8,128)(2,1)S(1)} %bitcast.131), channel_id=1, replica_groups=mesh['row'=16,'col'=4,'seq'=8] {'seq'}, dimensions={0} | all-to-all | bytes 1048576 | tf_op jit(solution)/shard_map/all_to_all | solution.py:121
  363.5 11.8 %all_to_all.106 = bf16[128,8,256]{2,1,0:T(8,128)(2,1)S(1)} all-to-all(bf16[128,8,256]{2,1,0:T(8,128)(2,1)S(1)} %copy.52), channel_id=1, replica_groups=mesh['row'=16,'col'=4,'seq'=8] {'col'}, dimensions={0} | all-to-all | bytes 1048576 | tf_op jit(solution)/shard_map/all_to_all | solution.py:115
  375.3 25.9 %all_to_all.107 = bf16[32,8,1024]{2,1,0:T(8,128)(2,1)S(1)} all-to-all(bf16[32,8,1024]{2,1,0:T(8,128)(2,1)S(1)} %bitcast.134), channel_id=1, replica_groups=mesh['row'=16,'col'=4,'seq'=8] {'seq'}, dimensions={0} | all-to-all | bytes 1048576 | tf_op jit(solution)/shard_map/all_to_all | solution.py:114
  401.2 153.9 %all-gather.4.cloned.1.call-done = bf16[4,1024,1024]{2,1,0:T(8,128)(2,1)} async-done(((bf16[4,64,1024]{2,1,0:T(8,128)(2,1)}), bf16[4,1024,1024]{2,1,0:T(8,128)(2,1)}) %all-gather.4.cloned.1.call-update) | async-done | bytes 8388624 | tf_op jit(solution)/shard_map/all_gather | solution.py:129
  555.1 6.0 convolution_convert_fusion
  562.7 13.3 %all_to_all.108 = bf16[4,2,32768]{2,1,0:T(2,128)(2,1)S(1)} all-to-all(bf16[4,2,32768]{2,1,0:T(2,128)(2,1)S(1)} %reshape.114), channel_id=1, replica_groups=mesh['row'=16,'col'=4,'seq'=8] {'col'}, dimensions={0} | all-to-all | bytes 1048576 | tf_op jit(solution)/shard_map/all_to_all | solution.py:132
  578.4 6.7 %all-to-all-start.6 = ((bf16[16,64,256]{2,0,1:T(8,128)(2,1)}), bf16[16,64,256]{2,0,1:T(8,128)(2,1)S(1)}, u32[]{:S(2)}, u32[]{:S(2)}) async-start(bf16[16,64,256]{2,0,1:T(8,128)(2,1)} %copy.61), calls=%async_computation.6 | async-start | bytes 1048576 | tf_op jit(solution)/shard_map/all_to_all | solution.py:131
  585.1 1.4 fusion.16
  586.5 16.9 %all-to-all-done.6 = bf16[16,64,256]{2,0,1:T(8,128)(2,1)S(1)} async-done(((bf16[16,64,256]{2,0,1:T(8,128)(2,1)}), bf16[16,64,256]{2,0,1:T(8,128)(2,1)S(1)}, u32[]{:S(2)}, u32[]{:S(2)}) %all-to-all-start.6) | async-done | bytes 524320 | tf_op jit(solution)/shard_map/all_to_all | solution.py:131
  604.1 2.4 fusion.19
  (79 shorter events, 24.2 us)
Async XLA Ops:
  7.4 318.0 %copy-start = (bf16[128,128]{1,0:T(8,128)(2,1)S(1)}, bf16[128,128]{1,0:T(8,128)(2,1)}, u32[]{:S(2)}) copy-start(bf16[128,128]{1,0:T(8,128)(2,1)} %param.21) | copy-start | bytes 98308
  30.8 20.2 %copy-start.2 = (bf16[1,256,256]{2,1,0:T(8,128)(2,1)S(1)}, bf16[1,256,256]{2,1,0:T(8,128)(2,1)}, u32[]{:S(2)}) copy-start(bf16[1,256,256]{2,1,0:T(8,128)(2,1)} %param.14) | copy-start | bytes 393220
  30.8 20.2 %copy-start.8 = (bf16[256,32]{0,1:T(8,128)(2,1)S(1)}, bf16[256,32]{0,1:T(8,128)(2,1)}, u32[]{:S(2)}) copy-start(bf16[256,32]{0,1:T(8,128)(2,1)} %param.16) | copy-start | bytes 49156
  33.6 70.2 %all-to-all-start = ((bf16[128,2,4096]{2,1,0:T(2,128)(2,1)}), bf16[128,2,4096]{2,1,0:T(2,128)(2,1)S(1)}, u32[]{:S(2)}, u32[]{:S(2)}) async-start(bf16[128,2,4096]{2,1,0:T(2,128)(2,1)} %reshape.112), calls=%async_computation | async-start | bytes 4194304 | tf_op jit(solution)/shard_map/all_to_all | solution.py:64
  51.0 239.5 %all-gather.6.cloned.1.call-start = ((), (), s32[]{:S(2)}) async-start(), calls=%async_computation.9 | async-start | bytes 4227072 | tf_op jit(solution)/shard_map/all_gather | solution.py:69
  52.2 250.5 %all-reduce.2.cloned.1.call-start = ((), (), s32[]{:S(2)}) async-start(), calls=%async_computation.7 | async-start | bytes 131072 | tf_op jit(solution)/shard_map/psum | solution.py:11
  112.5 442.6 %all-gather.4.cloned.1.call-start = ((), (), s32[]{:S(2)}) async-start(), calls=%async_computation.8 | async-start | bytes 8912896 | tf_op jit(solution)/shard_map/all_gather | solution.py:129
  112.5 190.1 %copy-start.1 = (bf16[1024,128]{1,0:T(8,128)(2,1)S(1)}, bf16[1024,128]{1,0:T(8,128)(2,1)}, u32[]{:S(2)}) copy-start(bf16[1024,128]{1,0:T(8,128)(2,1)} %param.17) | copy-start | bytes 786436
  323.8 2.0 copy-start.3
  325.8 36.5 %copy-start.6 = (bf16[128,128]{1,0:T(8,128)(2,1)S(1)}, bf16[128,128]{1,0:T(8,128)(2,1)}, u32[]{:S(2)}) copy-start(bf16[128,128]{1,0:T(8,128)(2,1)} %param.19) | copy-start | bytes 98308
  339.9 22.9 %copy-start.4 = (bf16[128,128]{1,0:T(8,128)(2,1)S(1)}, bf16[128,128]{1,0:T(8,128)(2,1)}, u32[]{:S(2)}) copy-start(bf16[128,128]{1,0:T(8,128)(2,1)} %param.18) | copy-start | bytes 98308
  561.8 23.3 %copy-start.5 = (bf16[128,128]{1,0:T(8,128)(2,1)S(1)}, bf16[128,128]{1,0:T(8,128)(2,1)}, u32[]{:S(2)}) copy-start(bf16[128,128]{1,0:T(8,128)(2,1)} %param.23) | copy-start | bytes 98308
  561.8 23.3 %copy-start.7 = (bf16[128,128]{1,0:T(8,128)(2,1)S(1)}, bf16[128,128]{1,0:T(8,128)(2,1)}, u32[]{:S(2)}) copy-start(bf16[128,128]{1,0:T(8,128)(2,1)} %param.22) | copy-start | bytes 98308
  578.4 25.1 %all-to-all-start.6 = ((bf16[16,64,256]{2,0,1:T(8,128)(2,1)}), bf16[16,64,256]{2,0,1:T(8,128)(2,1)S(1)}, u32[]{:S(2)}, u32[]{:S(2)}) async-start(bf16[16,64,256]{2,0,1:T(8,128)(2,1)} %copy.61), calls=%async_computation.6 | async-start | bytes 1048576 | tf_op jit(solution)/shard_map/all_to_all | solution.py:131
Sparse Core Ops, SparseCore 0:
  53.9 236.4 all-gather.5
Sparse Core Ops, SparseCore 1:
  112.5 47.5 all-reduce.1
  362.4 192.6 all-gather.3
